TPU v7x, 512 devices: a whole 4x4x16 slice. The times are simulated.
512 devices in a mesh: row: 16 (over z), col: 32 (over x, y, core).
Axes of the slice: x: 4, y: 4, z: 16, core: 2. Of those that a mesh axis runs over, the one named last changes fastest.
Arguments:
- children: float32 [2, 4096, 16384], P(None, 'row', 'col'), may hold values from -1 to 6, as said below
- block_maps: int32 [2, 64], replicated, may hold values from 0 to 63, each once within a row
Outputs:
- panel_rows: float32 [512, 16384], P(None, 'col')
- trailing: float32 [2, 4096, 16384], P(None, 'row', 'col')
Inputs may be any that keep to these rules, and one draw needn't show every extreme that they name: Each row of block_maps names every parent column block once. `children`: each child's block is upper triangular in its own column order: entry (i, j) is zero where j < i.
All inputs are finite; a program needn't handle non-finite values.
Results may differ from a plain program's by a relative error of at most 0.000078.
Values sent between devices are 32-bit elements; how exact they have to be, the bound alone decides.
A program may use at most 64 MiB of HBM per device.

v0:
```python
import jax
import jax.numpy as jnp
from jax import lax
from jax.sharding import PartitionSpec as P

PANEL = 256


def from_root(array, axis, root):
    mine = lax.axis_index(axis) == root
    return lax.psum(jnp.where(mine, array, jnp.zeros_like(array)), axis)


def crossed(left_matrix, right_matrix):
    return jnp.dot(
        left_matrix.T,
        right_matrix,
        precision=lax.Precision.HIGHEST,
        preferred_element_type=jnp.float32,
    )


def applied(left_matrix, right_matrix):
    return jnp.dot(
        left_matrix,
        right_matrix,
        precision=lax.Precision.HIGHEST,
        preferred_element_type=jnp.float32,
    )


def basis_from(panel_cols, factor):
    return lax.linalg.triangular_solve(
        factor, panel_cols, left_side=False, lower=True, transpose_a=True
    )


def inverted(mapping, block_count):
    return (
        jnp.zeros((block_count,), jnp.int32)
        .at[mapping]
        .set(jnp.arange(block_count, dtype=jnp.int32))
    )


def per_device(children, block_maps):
    rows_dev = children.shape[1]
    width_dev = children.shape[2]
    blocks_dev = width_dev // PANEL
    block_count = blocks_dev * lax.axis_size("col")
    first_inverse = inverted(block_maps[0], block_count)
    second_inverse = inverted(block_maps[1], block_count)
    tiles = children.reshape(2, rows_dev, blocks_dev, PANEL)
    spread = lax.all_to_all(tiles, "col", split_axis=1, concat_axis=2, tiled=True)
    moved = jnp.stack(
        [jnp.take(spread[0], first_inverse, axis=1), jnp.take(spread[1], second_inverse, axis=1)]
    )
    settled = lax.all_to_all(moved, "col", split_axis=2, concat_axis=1, tiled=True)
    front_rows = settled.reshape(2 * rows_dev, width_dev)
    both_panels = from_root(front_rows, "col", 0)
    panel_one = both_panels[:, :PANEL]
    panel_two = both_panels[:, PANEL:]
    factor_one = jnp.linalg.cholesky(lax.psum(crossed(panel_one, panel_one), "row"))
    basis_one = basis_from(panel_one, factor_one)
    coupling = lax.psum(crossed(basis_one, panel_two), "row")
    updated_two = panel_two - applied(basis_one, coupling)
    factor_two = jnp.linalg.cholesky(lax.psum(crossed(updated_two, updated_two), "row"))
    basis_two = basis_from(updated_two, factor_two)
    rows_one = lax.psum(crossed(basis_one, front_rows), "row")
    front_rows = front_rows - applied(basis_one, rows_one)
    rows_two = lax.psum(crossed(basis_two, front_rows), "row")
    front_rows = front_rows - applied(basis_two, rows_two)
    upper_rows = jnp.concatenate([rows_one, rows_two], axis=0)
    return (upper_rows, front_rows.reshape(2, rows_dev, width_dev))


def solution(mesh):
    placed = (P(None, "row", "col"), P())
    return jax.shard_map(
        per_device,
        mesh=mesh,
        in_specs=placed,
        out_specs=(P(None, "col"), P(None, "row", "col")),
        check_vma=False,
    )
```

profile of v0, /device:TPU:24, one launch (start us, length us, event | category | flops | bytes accessed | tf_op | source)
XLA Modules:
  0.0 881.4 jit_solution(15743211670340210446)
XLA Ops:
  10.0 9.2 %all-to-all-start = ((f32[2,256,2,256]{3,2,0,1:T(2,128)}), f32[2,256,2,256]{3,2,0,1:T(2,128)S(1)}, u32[]{:S(2)}, u32[]{:S(2)}) async-start(f32[2,256,2,256]{3,2,0,1:T(2,128)} %copy.27), calls=%async_computation | async-start | bytes 2097152 | tf_op jit(solution)/shard_map/all_to_all | solution.py:54
  21.6 13.1 %all-to-all-done = f32[2,256,2,256]{3,2,0,1:T(2,128)S(1)} async-done(((f32[2,256,2,256]{3,2,0,1:T(2,128)}), f32[2,256,2,256]{3,2,0,1:T(2,128)S(1)}, u32[]{:S(2)}, u32[]{:S(2)}) %all-to-all-start) | async-done | bytes 1048608 | tf_op jit(solution)/shard_map/all_to_all | solution.py:54
  37.9 5.5 all-to-all-start.1
  43.4 15.3 %all-to-all-done.1 = f32[2,8,64,256]{3,1,0,2:T(8,128)S(1)} async-done(((f32[2,8,64,256]{3,1,0,2:T(8,128)}), f32[2,8,64,256]{3,1,0,2:T(8,128)S(1)}, u32[]{:S(2)}, u32[]{:S(2)}) %all-to-all-start.1) | async-done | bytes 1048608 | tf_op jit(solution)/shard_map/all_to_all | solution.py:58
  60.0 136.4 %all-reduce.8.cloned.1.call-done = f32[512,512]{1,0:T(8,128)} async-done(((f32[512,512]{1,0:T(8,128)}), f32[512,512]{1,0:T(8,128)}) %all-reduce.8.cloned.1.call-update) | async-done | bytes 1048592 | tf_op jit(solution)/shard_map/psum | solution.py:11
  196.3 2.9 fusion
  199.6 135.0 %all-reduce.10.cloned.1.call-done = f32[256,256]{0,1:T(8,128)} async-done(((f32[256,256]{0,1:T(8,128)}), f32[256,256]{0,1:T(8,128)}) %all-reduce.10.cloned.1.call-update) | async-done | bytes 262160 | tf_op jit(solution)/shard_map/psum | solution.py:63
  335.9 11.7 %cholesky.130 = f32[128,128]{1,0:T(8,128)S(1)} custom-call(f32[128,128]{1,0:T(8,128)S(1)} %cholesky.194), custom_call_target="Cholesky" | custom-call | tf_op jit(solution)/shard_map/jit(cholesky)/cholesky | solution.py:63
  347.6 9.8 %custom-call.13 = f32[1,128,128]{1,2,0:T(8,128)S(1)} custom-call(f32[1,128,128]{2,1,0:T(8,128)S(1)} %get-tuple-element.52), custom_call_target="InvertDiagBlocksLowerTriangular" | custom-call | tf_op jit(solution)/shard_map/jit(cholesky)/cholesky | solution.py:63
  358.0 11.7 %cholesky.147 = f32[128,128]{1,0:T(8,128)S(1)} custom-call(f32[128,128]{1,0:T(8,128)S(1)} %convolution_subtract_fusion.6), custom_call_target="Cholesky" | custom-call | tf_op jit(solution)/shard_map/jit(cholesky)/cholesky | solution.py:63
  372.5 4.6 while.4
  377.2 19.7 %custom-call.14 = f32[2,128,128]{1,2,0:T(8,128)S(1)} custom-call(f32[2,128,128]{2,1,0:T(8,128)S(1)} %get-tuple-element.19), custom_call_target="InvertDiagBlocksLowerTriangular" | custom-call | tf_op jit(solution)/shard_map/triangular_solve/custom-call.0 | solution.py:33
  399.7 1.8 fusion.11
  401.5 130.7 %all-reduce.12.cloned.1.call-done = f32[256,256]{1,0:T(8,128)} async-done(((f32[256,256]{1,0:T(8,128)}), f32[256,256]{1,0:T(8,128)}) %all-reduce.12.cloned.1.call-update) | async-done | bytes 262160 | tf_op jit(solution)/shard_map/psum | solution.py:65
  532.2 1.9 convolution_subtract_fusion.2
  536.1 135.0 %all-reduce.16.cloned.1.call-done = (f32[256,512]{1,0:T(8,128)}, f32[256,256]{0,1:T(8,128)}) async-done(((f32[256,512]{1,0:T(8,128)}, f32[256,256]{0,1:T(8,128)}), (f32[256,512]{1,0:T(8,128)}, f32[256,256]{0,1:T(8,128)})) %all-reduce.16.cloned.1.call-update) | async-done | bytes 786448 | tf_op jit(solution)/shard_map/psum | solution.py:69
  672.3 11.7 %cholesky.164 = f32[128,128]{1,0:T(8,128)S(1)} custom-call(f32[128,128]{1,0:T(8,128)S(1)} %cholesky.197), custom_call_target="Cholesky" | custom-call | tf_op jit(solution)/shard_map/jit(cholesky)/cholesky | solution.py:67
  684.1 9.8 %custom-call.15 = f32[1,128,128]{1,2,0:T(8,128)S(1)} custom-call(f32[1,128,128]{2,1,0:T(8,128)S(1)} %get-tuple-element.48), custom_call_target="InvertDiagBlocksLowerTriangular" | custom-call | tf_op jit(solution)/shard_map/jit(cholesky)/cholesky | solution.py:67
  694.4 11.7 %cholesky.181 = f32[128,128]{1,0:T(8,128)S(1)} custom-call(f32[128,128]{1,0:T(8,128)S(1)} %convolution_subtract_fusion.5), custom_call_target="Cholesky" | custom-call | tf_op jit(solution)/shard_map/jit(cholesky)/cholesky | solution.py:67
  708.8 4.2 while.5
  713.0 19.7 %custom-call.16 = f32[2,128,128]{1,2,0:T(8,128)S(1)} custom-call(f32[2,128,128]{2,1,0:T(8,128)S(1)} %get-tuple-element.20), custom_call_target="InvertDiagBlocksLowerTriangular" | custom-call | tf_op jit(solution)/shard_map/triangular_solve/custom-call.0 | solution.py:33
  735.2 1.8 fusion.4
  737.1 133.4 %all-reduce.14.cloned.1.call-done = f32[256,512]{1,0:T(8,128)} async-done(((f32[256,512]{1,0:T(8,128)}), f32[256,512]{1,0:T(8,128)}) %all-reduce.14.cloned.1.call-update) | async-done | bytes 524304 | tf_op jit(solution)/shard_map/psum | solution.py:71
  870.5 3.1 convolution_subtract_fusion
  (95 shorter events, 32.5 us)
Async XLA Ops:
  10.0 24.6 %all-to-all-start = ((f32[2,256,2,256]{3,2,0,1:T(2,128)}), f32[2,256,2,256]{3,2,0,1:T(2,128)S(1)}, u32[]{:S(2)}, u32[]{:S(2)}) async-start(f32[2,256,2,256]{3,2,0,1:T(2,128)} %copy.27), calls=%async_computation | async-start | bytes 2097152 | tf_op jit(solution)/shard_map/all_to_all | solution.py:54
  19.2 0.7 copy-start.6
  37.9 20.8 %all-to-all-start.1 = ((f32[2,8,64,256]{3,1,0,2:T(8,128)}), f32[2,8,64,256]{3,1,0,2:T(8,128)S(1)}, u32[]{:S(2)}, u32[]{:S(2)}) async-start(f32[2,8,64,256]{3,1,0,2:T(8,128)} %copy.31), calls=%async_computation.1 | async-start | bytes 2097152 | tf_op jit(solution)/shard_map/all_to_all | solution.py:58
  43.4 153.0 %all-reduce.8.cloned.1.call-start = ((), (), s32[]{:S(2)}) async-start(), calls=%async_computation.2 | async-start | bytes 2097152 | tf_op jit(solution)/shard_map/psum | solution.py:11
  59.9 274.7 %all-reduce.10.cloned.1.call-start = ((), (), s32[]{:S(2)}) async-start(), calls=%async_computation.3 | async-start | bytes 524288 | tf_op jit(solution)/shard_map/psum | solution.py:63
  199.3 332.9 %all-reduce.12.cloned.1.call-start = ((), (), s32[]{:S(2)}) async-start(), calls=%async_computation.4 | async-start | bytes 524288 | tf_op jit(solution)/shard_map/psum | solution.py:65
  334.6 1.2 copy-start.5
  357.5 39.4 %copy-start = (f32[512,512]{1,0:T(8,128)S(1)}, f32[512,512]{1,0:T(8,128)}, u32[]{:S(2)}) copy-start(f32[512,512]{1,0:T(8,128)} %all-reduce.8.cloned.1.call-done) | copy-start | bytes 3145732
  399.6 271.5 %all-reduce.16.cloned.1.call-start = ((), (), s32[]{:S(2)}) async-start(), calls=%async_computation.6 | async-start | bytes 1572864 | tf_op jit(solution)/shard_map/psum | solution.py:69
  535.9 334.6 %all-reduce.14.cloned.1.call-start = ((), (), s32[]{:S(2)}) async-start(), calls=%async_computation.5 | async-start | bytes 1048576 | tf_op jit(solution)/shard_map/psum | solution.py:71
  671.1 1.2 copy-start.4
  733.1 1.0 copy-start.1
  737.0 136.6 %copy-start.2 = (f32[256,512]{1,0:T(8,128)S(1)}, f32[256,512]{1,0:T(8,128)}, u32[]{:S(2)}) copy-start(f32[256,512]{1,0:T(8,128)} %get-tuple-element.37) | copy-start | bytes 1572868
  870.5 3.1 copy-start.3
Sparse Core Ops, SparseCore 0:
  60.1 136.2 all-reduce.7
  199.4 135.2 all-reduce.9
  399.8 132.3 all-reduce.11
  536.0 135.0 all-reduce.15
  737.2 133.2 all-reduce.13
where the time goes:
time: 886 us; the launch traced here: 881 us
  waiting for transfers between devices  699 us (79%)
  other arithmetic  111 us (13%)
  matrix products  19.5 us (2%)
  local copies, waits for them, and re-layouts  18.5 us (2%)
  between operations  17.1 us (2%)
  starting transfers between devices  15.4 us (2%)
    psum x1, waiting for transfers between devices, from_root(): return lax.psum(jnp.where(mine, array, jnp.zeros_like(array)), axis)  136 us
    psum x1, waiting for transfers between devices, per_device(): lax.psum(crossed(panel_one, panel_one), 'row')  135 us
    psum x1, waiting for transfers between devices, per_device(): rows_one = lax.psum(crossed(basis_one, front_rows), 'row')  135 us
    psum x1, waiting for transfers between devices, per_device(): rows_two = lax.psum(crossed(basis_two, front_rows), 'row')  133 us
    psum x1, waiting for transfers between devices, per_device(): coupling = lax.psum(crossed(basis_one, panel_two), 'row')  131 us
    another operation x5, other arithmetic, basis_from(): lax.linalg.triangular_solve(factor, panel_cols, left_side=False, lower=Tr...  39.4 us
    another operation x7, other arithmetic, per_device(): jnp.linalg.cholesky(lax.psum(crossed(panel_one, panel_one), 'row'))  34.7 us
    another operation x7, other arithmetic, per_device(): jnp.linalg.cholesky(lax.psum(crossed(updated_two, updated_two), 'row'))  34.6 us
  transfers between devices with their start and end apart: 7, of which 7 were waited for; matrix products, arithmetic and copies ran while one was open for 0% of the time, Pallas kernels for 0%

commit v1 on v0

v1 whole, which is shorter than its diff:
```python
import functools

import jax
import jax.numpy as jnp
from jax import lax
from jax.experimental import pallas as pl
from jax.experimental.pallas import tpu as pltpu
from jax.sharding import PartitionSpec as P

PANEL = 256
WIDE = 2 * PANEL
F32 = jnp.float32
BF16 = jnp.bfloat16
MESH = pl.DeviceIdType.MESH
VMEM = pl.BlockSpec(memory_space=pltpu.VMEM)
SMEM = pl.BlockSpec(memory_space=pltpu.SMEM)


def split(x):
    high = x.astype(BF16)
    low = (x - high.astype(F32)).astype(BF16)
    return high, low


def product(a, b, dims=((1,), (0,))):
    def one(x, y):
        return lax.dot_general(x, y, (dims, ((), ())), preferred_element_type=F32)

    return one(a[0], b[0]) + (one(a[0], b[1]) + one(a[1], b[0]))


def exchange_kernel(ncol, rows, inv_ref, kids_ref, front_ref, panel_ref, got, out, sems):
    me = lax.axis_index("col")
    barrier = pltpu.get_barrier_semaphore()

    @pl.loop(1, ncol)
    def _(d):
        pl.semaphore_signal(barrier, inc=1, device_id={"col": lax.rem(me + d, ncol)}, device_id_type=MESH)

    pl.semaphore_wait(barrier, ncol - 1)

    def send(src, dst, phase, to):
        pltpu.make_async_remote_copy(
            src_ref=src,
            dst_ref=dst,
            send_sem=sems.at[2 * phase],
            recv_sem=sems.at[2 * phase + 1],
            device_id={"col": to},
            device_id_type=MESH,
        ).start()

    def drain(ref, which):
        pltpu.make_async_copy(ref, ref, sems.at[which]).wait()

    def slab(owner):
        return pl.ds(pl.multiple_of(owner * rows, rows), rows)

    @pl.loop(1, ncol)
    def _(d):
        to = lax.rem(me + d, ncol)
        send(kids_ref.at[:, slab(to), :], got.at[me], 0, to)

    got[me] = kids_ref[:, slab(me), :]
    many = out.at[pl.ds(0, ncol - 1)]
    drain(got.at[pl.ds(0, ncol - 1)], 1)

    def place(to):
        for child in range(2):
            for half in range(2):
                block = inv_ref[child, 2 * to + half]
                pair = got[block // 2, child]
                low = jnp.broadcast_to(lax.rem(block, 2), (rows, PANEL)) == 0
                out[to, child, :, half * PANEL : (half + 1) * PANEL] = jnp.where(
                    low, pair[:, :PANEL], pair[:, PANEL:]
                )

    place(0)

    @pl.loop(1, ncol)
    def _(d):
        to = lax.rem(me + d, ncol)
        send(out.at[0], panel_ref.at[:, slab(me), :], 1, to)

    panel_ref[:, slab(me), :] = out[0]

    @pl.loop(1, ncol)
    def _(to):
        place(to)

    @pl.loop(1, ncol)
    def _(d):
        to = lax.rem(me + d, ncol)
        send(out.at[to], front_ref.at[:, slab(me), :], 2, to)

    front_ref[:, slab(me), :] = out[me]
    drain(many, 0)
    drain(many, 2)
    drain(many, 3)
    drain(many, 4)
    drain(many, 5)


def exchange(children, inverse, ncol):
    rows_dev = children.shape[1]
    rows = rows_dev // ncol
    piece = jax.ShapeDtypeStruct((2, rows_dev, WIDE), F32)
    return pl.pallas_call(
        functools.partial(exchange_kernel, ncol, rows),
        out_shape=(piece, piece),
        in_specs=[SMEM, VMEM],
        out_specs=(VMEM, VMEM),
        scratch_shapes=[
            pltpu.VMEM((ncol, 2, rows, WIDE), F32),
            pltpu.VMEM((ncol, 2, rows, WIDE), F32),
            pltpu.SemaphoreType.DMA((6,)),
        ],
        compiler_params=pltpu.CompilerParams(
            collective_id=0, has_side_effects=True, vmem_limit_bytes=32 << 20
        ),
        name="exchange",
    )(inverse, children)


def eliminate(gram, linv, base, k):
    top = pl.multiple_of(8 * k, 8)
    rows = gram[pl.ds(top, 8), :]
    inv_rows = linv[pl.ds(top, 8), :]
    turned = pltpu.roll(rows, lax.rem(128 - 8 * k, 128), axis=1)
    cols = [jnp.broadcast_to(turned[:, j : j + 1], (8, 128)) for j in range(8)]
    sub = lax.broadcasted_iota(jnp.int32, (8, 128), 0)
    for p in range(8):
        pivot = jnp.broadcast_to(cols[p][p : p + 1, :], (8, 128))
        recip = 1.0 / pivot
        root = lax.rsqrt(pivot)
        mult = jnp.where(sub > p, cols[p] * recip, 0.0)
        for j in range(p + 1, 8):
            cols[j] = cols[j] - mult * jnp.broadcast_to(cols[p][j : j + 1, :], (8, 128))
        row = jnp.broadcast_to(rows[p : p + 1, :], (8, 128))
        inv_row = jnp.broadcast_to(inv_rows[p : p + 1, :], (8, 128))
        scale = jnp.where(sub == p, root, 1.0)
        rows = (rows - mult * row) * scale
        inv_rows = (inv_rows - mult * inv_row) * scale
    gram[pl.ds(top, 8), :] = rows
    linv[pl.ds(top, 8), :] = inv_rows
    both = jnp.concatenate([rows, inv_rows], axis=1)
    update = lax.dot_general(
        rows, both, (((0,), (0,)), ((), ())), precision=lax.Precision.HIGHEST, preferred_element_type=F32
    )
    below = lax.broadcasted_iota(jnp.int32, (128, 128), 0) >= top + 8
    gram[...] = gram[...] - jnp.where(below, update[:, :128], 0.0)
    linv[...] = linv[...] - jnp.where(below, update[:, 128:], 0.0)


def reduce_kernel(
    nrow, ncol, front_ref, panel_ref, s_ref, linv_ref,
    local, gram, tiles, part, up, down, diag, dinv, sems, ring
):
    me = lax.axis_index("col")
    mz = lax.axis_index("row")
    strip = WIDE // ncol
    chunk = WIDE // nrow
    ntile = strip // 8 * (WIDE // 128)
    barrier = pltpu.get_barrier_semaphore()

    @pl.loop(1, ncol)
    def _(d):
        pl.semaphore_signal(barrier, inc=1, device_id={"col": lax.rem(me + d, ncol)}, device_id_type=MESH)

    @pl.loop(1, nrow)
    def _(d):
        pl.semaphore_signal(barrier, inc=1, device_id={"row": lax.rem(mz + d, nrow)}, device_id_type=MESH)

    pan = panel_ref[...].reshape(-1, WIDE)
    pan_t = split(pan.T)
    local[...] = product(pan_t, split(pan))
    pl.semaphore_wait(barrier, ncol + nrow - 2)

    def send(src, dst, sem, phase, to):
        pltpu.make_async_remote_copy(
            src_ref=src,
            dst_ref=dst,
            send_sem=sem.at[2 * phase],
            recv_sem=sem.at[2 * phase + 1],
            device_id=to,
            device_id_type=MESH,
        ).start()

    def drain(ref, sem, which):
        pltpu.make_async_copy(ref, ref, sem.at[which]).wait()

    def tile_at(z):
        t = lax.rem(z, ntile)
        top = me * strip + (t // 4) * 8
        return pl.ds(pl.multiple_of(top, 8), 8), pl.ds(pl.multiple_of(lax.rem(t, 4) * 128, 128), 128)

    def my_strip():
        return pl.ds(pl.multiple_of(me * strip, 8), strip)

    @pl.loop(1, nrow)
    def _(d):
        to = lax.rem(mz + d, nrow)
        r, c = tile_at(to)
        send(local.at[r, c], tiles.at[mz], sems, 0, {"row": to})

    r, c = tile_at(mz)
    tiles[mz] = local[r, c]
    drain(tiles.at[pl.ds(0, nrow - 1)], sems, 1)
    total = tiles[0]
    for z in range(1, nrow):
        total = total + tiles[z]
    gram[r, c] = total
    offsets = [d for d in range(-(ntile // 2), ntile // 2) if d]
    for d in offsets:
        send(gram.at[r, c], gram.at[r, c], sems, 1, {"row": lax.rem(mz + d + nrow, nrow)})
    fr = split(front_ref[...].reshape(-1, WIDE))
    whole = product(pan_t, fr)
    part[...] = whole.reshape(nrow, chunk, WIDE)
    drain(tiles.at[pl.ds(0, ntile - 1)], sems, 3)

    @pl.loop(1, ncol)
    def _(d):
        to = lax.rem(me + d, ncol)
        send(gram.at[my_strip(), :], gram.at[my_strip(), :], sems, 2, {"col": to})

    half = nrow // 2
    after = {"row": lax.rem(mz + 1, nrow)}
    before = {"row": lax.rem(mz + nrow - 1, nrow)}

    def at(offset):
        return lax.rem(mz + offset + 2 * nrow, nrow)

    def copy(src, dst, index, to):
        return pltpu.make_async_remote_copy(
            src_ref=src, dst_ref=dst, send_sem=ring.at[0, index], recv_sem=ring.at[1, index],
            device_id=to, device_id_type=MESH,
        )

    def scatter_down(s):
        src = part.at[at(-half)] if s == 0 else down.at[s - 1]
        return copy(src, down.at[s], s, before)

    def scatter_up(s):
        src = part.at[at(half - 1)] if s == 0 else up.at[s - 1]
        return copy(src, up.at[s], half + s, after)

    def gather_up(s):
        here = s_ref.at[at(-s)]
        return copy(here, here, 2 * half + s, after)

    def gather_down(s):
        here = s_ref.at[at(s)]
        return copy(here, here, 3 * half + s, before)

    def ring_step(s):
        if s == 0:
            scatter_down(0).start()
            scatter_up(0).start()
        elif s < half:
            scatter_down(s - 1).wait()
            down[s - 1] = down[s - 1] + part[at(s - half)]
            scatter_down(s).start()
            scatter_up(s - 1).wait()
            if s < half - 1:
                up[s - 1] = up[s - 1] + part[at(half - 1 - s)]
                scatter_up(s).start()
        elif s == half:
            scatter_down(half - 1).wait()
            s_ref[mz] = part[mz] + up[half - 2] + down[half - 1]
            gather_up(0).start()
            gather_down(0).start()
        else:
            q = s - half
            gather_up(q - 1).wait()
            if q < half:
                gather_up(q).start()
            if q < half:
                gather_down(q - 1).wait()
                if q < half - 1:
                    gather_down(q).start()

    ring_step(0)
    drain(gram.at[pl.ds(0, WIDE - strip), :], sems, 5)
    drain(tiles.at[pl.ds(0, ntile - 1)], sems, 2)
    drain(gram.at[pl.ds(0, WIDE - strip), :], sems, 4)
    linv_ref[...] = jnp.zeros((WIDE, WIDE), F32)
    row_id = lax.broadcasted_iota(jnp.int32, (128, 128), 0)
    col_id = lax.broadcasted_iota(jnp.int32, (128, 128), 1)
    eye = jnp.where(row_id == col_id, 1.0, 0.0)
    step = 1
    for ob in range(WIDE // 128):
        lo, hi = 128 * ob, 128 * (ob + 1)
        diag[...] = gram[lo:hi, lo:hi]
        dinv[...] = eye
        for quarter in range(4):

            @pl.loop(0, 4)
            def _(i):
                eliminate(diag, dinv, ob, 4 * quarter + i)

            if step <= 2 * half:
                ring_step(step)
                step += 1
        inv = split(jnp.where(row_id >= col_id, dinv[...], 0.0))
        linv_ref[lo:hi, lo:hi] = jnp.where(row_id >= col_id, dinv[...], 0.0)
        if ob:
            linv_ref[lo:hi, :lo] = product(inv, split(linv_ref[lo:hi, :lo]))
        if hi < WIDE:
            right = product(inv, split(gram[lo:hi, hi:]))
            right_t = split(right.T)
            gram[hi:, hi:] = gram[hi:, hi:] - product(right_t, split(right))
            linv_ref[hi:, :hi] = linv_ref[hi:, :hi] - product(right_t, split(linv_ref[lo:hi, :hi]))
    while step <= 2 * half:
        ring_step(step)
        step += 1
    drain(tiles.at[pl.ds(0, nrow - 1)], sems, 0)


def reduced(front, panel, nrow, ncol):
    chunk = WIDE // nrow
    half = nrow // 2
    return pl.pallas_call(
        functools.partial(reduce_kernel, nrow, ncol),
        out_shape=(
            jax.ShapeDtypeStruct((nrow, chunk, WIDE), F32),
            jax.ShapeDtypeStruct((WIDE, WIDE), F32),
        ),
        in_specs=[VMEM, VMEM],
        out_specs=(VMEM, VMEM),
        scratch_shapes=[
            pltpu.VMEM((WIDE, WIDE), F32),
            pltpu.VMEM((WIDE, WIDE), F32),
            pltpu.VMEM((nrow, 8, 128), F32),
            pltpu.VMEM((nrow, chunk, WIDE), F32),
            pltpu.VMEM((half - 1, chunk, WIDE), F32),
            pltpu.VMEM((half, chunk, WIDE), F32),
            pltpu.VMEM((128, 128), F32),
            pltpu.VMEM((128, 128), F32),
            pltpu.SemaphoreType.DMA((6,)),
            pltpu.SemaphoreType.DMA((2, 4 * half)),
        ],
        compiler_params=pltpu.CompilerParams(
            collective_id=1, has_side_effects=True, vmem_limit_bytes=48 << 20
        ),
        name="reduce_and_factor",
    )(front, panel)


def finish_kernel(front_ref, panel_ref, s_ref, linv_ref, rows_ref, trail_ref):
    inv = split(linv_ref[...])
    upper = product(inv, split(s_ref[...].reshape(WIDE, WIDE)))
    rows_ref[...] = upper
    back = product(split(linv_ref[...].T), split(upper))
    pan = panel_ref[...].reshape(-1, WIDE)
    trail_ref[...] = front_ref[...] - product(split(pan), split(back)).reshape(front_ref.shape)


def finish(front, panel, s, linv):
    return pl.pallas_call(
        finish_kernel,
        out_shape=(
            jax.ShapeDtypeStruct((WIDE, WIDE), F32),
            jax.ShapeDtypeStruct(front.shape, F32),
        ),
        in_specs=[VMEM] * 4,
        out_specs=(VMEM, VMEM),
        compiler_params=pltpu.CompilerParams(vmem_limit_bytes=48 << 20),
        name="finish",
    )(front, panel, s, linv)


def inverted(maps):
    count = maps.shape[1]
    ids = lax.broadcasted_iota(jnp.int32, (2, count, count), 1)
    hit = maps[:, :, None] == lax.broadcasted_iota(jnp.int32, (2, count, count), 2)
    return jnp.sum(jnp.where(hit, ids, 0), axis=1)


def per_device(children, block_maps):
    ncol = lax.axis_size("col")
    nrow = lax.axis_size("row")
    front, panel = exchange(children, inverted(block_maps), ncol)
    s, linv = reduced(front, panel, nrow, ncol)
    return finish(front, panel, s, linv)


def solution(mesh):
    placed = (P(None, "row", "col"), P())
    return jax.shard_map(
        per_device,
        mesh=mesh,
        in_specs=placed,
        out_specs=(P(None, "col"), P(None, "row", "col")),
        check_vma=False,
    )
```

time: 886 us -> 162 us (0.18)
  waiting for transfers between devices: 699 us -> 0 us
  Pallas kernels: 0 us -> 159 us
  other arithmetic: 111 us -> 0.77 us
  matrix products: 19.5 us -> 0 us
  local copies, waits for them, and re-layouts: 18.5 us -> 1.22 us
  between operations: 17.1 us -> 0.65 us
  starting transfers between devices: 15.4 us -> 0 us
    psum x5 -> x0, waiting for transfers between devices: 670 us -> none  [the longest x1 136 us: from_root(): return lax.psum(jnp.where(mine, array, jnp.zeros_like(array)), axis)]
    pallas_call x0 -> x3, Pallas kernels: none -> 159 us  [the longest x1 101 us: reduced(): pl.pallas_call(functools.partial(reduce_kernel, nrow, ncol), out_shape=(j...]
    another operation x22 -> x0, other arithmetic: 109 us -> none  [the longest x5 39.4 us: basis_from(): lax.linalg.triangular_solve(factor, panel_cols, left_side=False, lower=Tr...]
    all_to_all x2 -> x0, waiting for transfers between devices: 28.4 us -> none  [the longest x1 15.3 us: per_device(): lax.all_to_all(moved, 'col', split_axis=2, concat_axis=1, tiled=True)]
    dot_general x8 -> x0, matrix products: 15.7 us -> none  [the longest x5 9.59 us: crossed(): jnp.dot(left_matrix.T, right_matrix, precision=lax.Precision.HIGHEST, pre...]
    all_to_all x2 -> x0, starting transfers between devices: 14.7 us -> none  [the longest x1 9.21 us: per_device(): lax.all_to_all(tiles, 'col', split_axis=1, concat_axis=2, tiled=True)]
    another operation x20 -> x0, local copies, waits for them, and re-layouts: 9.27 us -> none  [the longest x15 8.1 us: basis_from(): lax.linalg.triangular_solve(factor, panel_cols, left_side=False, lower=Tr...]
  transfers between devices with their start and end apart: 7 -> 0, of which waited for: 7 -> 0; matrix products, arithmetic and copies ran while one was open for 0% -> 0% of each run, Pallas kernels for 0% -> 0%
where the time goes in v1:
time: 162 us
  Pallas kernels  159 us (98%)
    pallas_call x1, Pallas kernels, reduced(): pl.pallas_call(functools.partial(reduce_kernel, nrow, ncol), out_shape=(j...  101 us
    pallas_call x1, Pallas kernels, exchange(): pl.pallas_call(functools.partial(exchange_kernel, ncol, rows), out_shape=...  53.9 us
    pallas_call x1, Pallas kernels, finish(): pl.pallas_call(finish_kernel, out_shape=(jax.ShapeDtypeStruct((WIDE, WIDE...  3.77 us

profile of v1, /device:TPU:24, one launch (start us, length us, event | category | flops | bytes accessed | tf_op | source)
XLA Modules:
  0.0 161.6 jit_solution(9229199903644841935)
XLA Ops:
  0.6 0.8 select_reduce_fusion.inv_ref
  1.4 0.0 copy-start
  1.4 1.2 copy-done
  2.6 53.9 %exchange.1 = (f32[2,256,512]{2,1,0:T(8,128)S(1)}, f32[2,256,512]{2,1,0:T(8,128)S(1)}) custom-call(s32[2,64]{1,0:T(2,128)S(1)} %select_reduce_fusion.inv_ref, f32[2,256,512]{2,1,0:T(8,128)S(1)} %copy-done), custom_call_target="tpu_custom_call" | custom-call | tf_op jit(solution)/shard_map/exchange/pallas_call | solution.py:107
  56.5 101.3 %reduce_and_factor.1 = (f32[16,32,512]{2,1,0:T(8,128)S(1)}, f32[512,512]{1,0:T(8,128)S(1)}) custom-call(f32[2,256,512]{2,1,0:T(8,128)S(1)} %get-tuple-element.6.front_ref, f32[2,256,512]{2,1,0:T(8,128)S(1)} %get-tuple-element.7.panel_ref), custom_call_target="tpu_custom_call" | custom-call | tf_op jit(solution)/shard_map/reduce_and_factor/pallas_call | solution.py:321
  157.9 3.8 %finish.1 = (f32[512,512]{1,0:T(8,128)}, f32[2,256,512]{2,1,0:T(8,128)}) custom-call(f32[2,256,512]{2,1,0:T(8,128)S(1)} %get-tuple-element.6.front_ref, f32[2,256,512]{2,1,0:T(8,128)S(1)} %get-tuple-element.7.panel_ref, f32[16,32,512]{2,1,0:T(8,128)S(1)} %get-tuple-element.8.s_ref, f32[512,512]{1,0:T(8,128)S(1)} %get-tuple-element.9.linv_ref), custom_call_target="tpu_custom_call" | custom-call | tf_op jit(solution)/shard_map/finish/pallas_call | solution.py:358
Async XLA Ops:
  1.4 1.2 copy-start

commit v2 on v1

--- a/solution.py
+++ b/solution.py
@@ -27,98 +27,6 @@
         return lax.dot_general(x, y, (dims, ((), ())), preferred_element_type=F32)
 
     return one(a[0], b[0]) + (one(a[0], b[1]) + one(a[1], b[0]))
-
-
-def exchange_kernel(ncol, rows, inv_ref, kids_ref, front_ref, panel_ref, got, out, sems):
-    me = lax.axis_index("col")
-    barrier = pltpu.get_barrier_semaphore()
-
-    @pl.loop(1, ncol)
-    def _(d):
-        pl.semaphore_signal(barrier, inc=1, device_id={"col": lax.rem(me + d, ncol)}, device_id_type=MESH)
-
-    pl.semaphore_wait(barrier, ncol - 1)
-
-    def send(src, dst, phase, to):
-        pltpu.make_async_remote_copy(
-            src_ref=src,
-            dst_ref=dst,
-            send_sem=sems.at[2 * phase],
-            recv_sem=sems.at[2 * phase + 1],
-            device_id={"col": to},
-            device_id_type=MESH,
-        ).start()
-
-    def drain(ref, which):
-        pltpu.make_async_copy(ref, ref, sems.at[which]).wait()
-
-    def slab(owner):
-        return pl.ds(pl.multiple_of(owner * rows, rows), rows)
-
-    @pl.loop(1, ncol)
-    def _(d):
-        to = lax.rem(me + d, ncol)
-        send(kids_ref.at[:, slab(to), :], got.at[me], 0, to)
-
-    got[me] = kids_ref[:, slab(me), :]
-    many = out.at[pl.ds(0, ncol - 1)]
-    drain(got.at[pl.ds(0, ncol - 1)], 1)
-
-    def place(to):
-        for child in range(2):
-            for half in range(2):
-                block = inv_ref[child, 2 * to + half]
-                pair = got[block // 2, child]
-                low = jnp.broadcast_to(lax.rem(block, 2), (rows, PANEL)) == 0
-                out[to, child, :, half * PANEL : (half + 1) * PANEL] = jnp.where(
-                    low, pair[:, :PANEL], pair[:, PANEL:]
-                )
-
-    place(0)
-
-    @pl.loop(1, ncol)
-    def _(d):
-        to = lax.rem(me + d, ncol)
-        send(out.at[0], panel_ref.at[:, slab(me), :], 1, to)
-
-    panel_ref[:, slab(me), :] = out[0]
-
-    @pl.loop(1, ncol)
-    def _(to):
-        place(to)
-
-    @pl.loop(1, ncol)
-    def _(d):
-        to = lax.rem(me + d, ncol)
-        send(out.at[to], front_ref.at[:, slab(me), :], 2, to)
-
-    front_ref[:, slab(me), :] = out[me]
-    drain(many, 0)
-    drain(many, 2)
-    drain(many, 3)
-    drain(many, 4)
-    drain(many, 5)
-
-
-def exchange(children, inverse, ncol):
-    rows_dev = children.shape[1]
-    rows = rows_dev // ncol
-    piece = jax.ShapeDtypeStruct((2, rows_dev, WIDE), F32)
-    return pl.pallas_call(
-        functools.partial(exchange_kernel, ncol, rows),
-        out_shape=(piece, piece),
-        in_specs=[SMEM, VMEM],
-        out_specs=(VMEM, VMEM),
-        scratch_shapes=[
-            pltpu.VMEM((ncol, 2, rows, WIDE), F32),
-            pltpu.VMEM((ncol, 2, rows, WIDE), F32),
-            pltpu.SemaphoreType.DMA((6,)),
-        ],
-        compiler_params=pltpu.CompilerParams(
-            collective_id=0, has_side_effects=True, vmem_limit_bytes=32 << 20
-        ),
-        name="exchange",
-    )(inverse, children)
 
 
 def eliminate(gram, linv, base, k):
@@ -151,15 +59,19 @@
     linv[...] = linv[...] - jnp.where(below, update[:, 128:], 0.0)
 
 
-def reduce_kernel(
-    nrow, ncol, front_ref, panel_ref, s_ref, linv_ref,
-    local, gram, tiles, part, up, down, diag, dinv, sems, ring
+def merge_kernel(
+    nrow, ncol, inv_ref, kids_ref, front_ref, panel_ref, s_ref, linv_ref,
+    got, out, local, gram, tiles, part, up, down, diag, dinv, sems, ring
 ):
     me = lax.axis_index("col")
     mz = lax.axis_index("row")
+    rows = kids_ref.shape[1] // ncol
     strip = WIDE // ncol
     chunk = WIDE // nrow
     ntile = strip // 8 * (WIDE // 128)
+    core = lax.rem(me, 2)
+    twin = me + 1 - 2 * core
+    chips = ncol // 2
     barrier = pltpu.get_barrier_semaphore()
 
     @pl.loop(1, ncol)
@@ -169,58 +81,108 @@
     @pl.loop(1, nrow)
     def _(d):
         pl.semaphore_signal(barrier, inc=1, device_id={"row": lax.rem(mz + d, nrow)}, device_id_type=MESH)
+
+    pl.semaphore_wait(barrier, ncol + nrow - 2)
+
+    def send(src, dst, phase, to):
+        pltpu.make_async_remote_copy(
+            src_ref=src,
+            dst_ref=dst,
+            send_sem=sems.at[2 * phase],
+            recv_sem=sems.at[2 * phase + 1],
+            device_id=to,
+            device_id_type=MESH,
+        ).start()
+
+    def drain(ref, which):
+        pltpu.make_async_copy(ref, ref, sems.at[which]).wait()
+
+    def slab(owner):
+        return pl.ds(pl.multiple_of(owner * rows, rows), rows)
+
+    def strip_of(owner):
+        return pl.ds(pl.multiple_of(owner * strip, strip), strip)
+
+    @pl.loop(1, ncol)
+    def _(d):
+        to = lax.rem(me + d, ncol)
+        send(kids_ref.at[:, slab(to), :], got.at[me], 0, {"col": to})
+
+    got[me] = kids_ref[:, slab(me), :]
+    drain(got.at[pl.ds(0, ncol - 1)], 1)
+
+    def place(to):
+        for child in range(2):
+            for half in range(2):
+                block = inv_ref[child, 2 * to + half]
+                pair = got[block // 2, child]
+                low = jnp.broadcast_to(lax.rem(block, 2), (rows, PANEL)) == 0
+                out[to, child, :, half * PANEL : (half + 1) * PANEL] = jnp.where(
+                    low, pair[:, :PANEL], pair[:, PANEL:]
+                )
+
+    place(0)
+
+    @pl.loop(1, chips)
+    def _(d):
+        send(out.at[0], panel_ref.at[:, slab(me), :], 1, {"col": lax.rem(me + 2 * d, ncol)})
+
+    panel_ref[:, slab(me), :] = out[0]
+
+    @pl.loop(1, ncol)
+    def _(to):
+        place(to)
+
+    @pl.loop(1, ncol)
+    def _(d):
+        to = lax.rem(me + d, ncol)
+        send(out.at[to], front_ref.at[:, slab(me), :], 2, {"col": to})
+
+    front_ref[:, slab(me), :] = out[me]
+    drain(out.at[pl.ds(0, chips - 1)], 3)
+
+    @pl.loop(0, chips)
+    def _(i):
+        here = panel_ref.at[:, slab(2 * i + core), :]
+        send(here, here, 3, {"col": twin})
+
+    drain(out.at[pl.ds(0, chips)], 7)
 
     pan = panel_ref[...].reshape(-1, WIDE)
     pan_t = split(pan.T)
     local[...] = product(pan_t, split(pan))
-    pl.semaphore_wait(barrier, ncol + nrow - 2)
-
-    def send(src, dst, sem, phase, to):
-        pltpu.make_async_remote_copy(
-            src_ref=src,
-            dst_ref=dst,
-            send_sem=sem.at[2 * phase],
-            recv_sem=sem.at[2 * phase + 1],
-            device_id=to,
-            device_id_type=MESH,
-        ).start()
-
-    def drain(ref, sem, which):
-        pltpu.make_async_copy(ref, ref, sem.at[which]).wait()
 
     def tile_at(z):
         t = lax.rem(z, ntile)
         top = me * strip + (t // 4) * 8
         return pl.ds(pl.multiple_of(top, 8), 8), pl.ds(pl.multiple_of(lax.rem(t, 4) * 128, 128), 128)
 
-    def my_strip():
-        return pl.ds(pl.multiple_of(me * strip, 8), strip)
-
     @pl.loop(1, nrow)
     def _(d):
         to = lax.rem(mz + d, nrow)
         r, c = tile_at(to)
-        send(local.at[r, c], tiles.at[mz], sems, 0, {"row": to})
+        send(local.at[r, c], tiles.at[mz], 4, {"row": to})
 
     r, c = tile_at(mz)
     tiles[mz] = local[r, c]
-    drain(tiles.at[pl.ds(0, nrow - 1)], sems, 1)
+    drain(tiles.at[pl.ds(0, nrow - 1)], 9)
     total = tiles[0]
     for z in range(1, nrow):
         total = total + tiles[z]
     gram[r, c] = total
-    offsets = [d for d in range(-(ntile // 2), ntile // 2) if d]
-    for d in offsets:
-        send(gram.at[r, c], gram.at[r, c], sems, 1, {"row": lax.rem(mz + d + nrow, nrow)})
+    for d in range(-(ntile // 2), ntile // 2):
+        if d:
+            send(gram.at[r, c], gram.at[r, c], 5, {"row": lax.rem(mz + d + nrow, nrow)})
+    drain(tiles.at[pl.ds(0, ntile - 1)], 11)
+
+    @pl.loop(1, chips)
+    def _(d):
+        here = gram.at[strip_of(me), :]
+        send(here, here, 6, {"col": lax.rem(me + 2 * d, ncol)})
+
+    drain(out.at[pl.ds(0, ncol - 1)], 5)
     fr = split(front_ref[...].reshape(-1, WIDE))
-    whole = product(pan_t, fr)
-    part[...] = whole.reshape(nrow, chunk, WIDE)
-    drain(tiles.at[pl.ds(0, ntile - 1)], sems, 3)
-
-    @pl.loop(1, ncol)
-    def _(d):
-        to = lax.rem(me + d, ncol)
-        send(gram.at[my_strip(), :], gram.at[my_strip(), :], sems, 2, {"col": to})
+    part[...] = product(pan_t, fr).reshape(nrow, chunk, WIDE)
 
     half = nrow // 2
     after = {"row": lax.rem(mz + 1, nrow)}
@@ -279,9 +241,17 @@
                     gather_down(q).start()
 
     ring_step(0)
-    drain(gram.at[pl.ds(0, WIDE - strip), :], sems, 5)
-    drain(tiles.at[pl.ds(0, ntile - 1)], sems, 2)
-    drain(gram.at[pl.ds(0, WIDE - strip), :], sems, 4)
+    drain(out.at[pl.ds(0, chips - 1)], 13)
+
+    @pl.loop(0, chips)
+    def _(i):
+        here = gram.at[strip_of(2 * i + core), :]
+        send(here, here, 7, {"col": twin})
+
+    drain(out.at[pl.ds(0, chips)], 15)
+    drain(out.at[pl.ds(0, chips)], 14)
+    drain(out.at[pl.ds(0, chips - 1)], 12)
+    drain(tiles.at[pl.ds(0, ntile - 1)], 10)
     linv_ref[...] = jnp.zeros((WIDE, WIDE), F32)
     row_id = lax.broadcasted_iota(jnp.int32, (128, 128), 0)
     col_id = lax.broadcasted_iota(jnp.int32, (128, 128), 1)
@@ -312,21 +282,32 @@
     while step <= 2 * half:
         ring_step(step)
         step += 1
-    drain(tiles.at[pl.ds(0, nrow - 1)], sems, 0)
-
-
-def reduced(front, panel, nrow, ncol):
+    drain(tiles.at[pl.ds(0, nrow - 1)], 8)
+    drain(out.at[pl.ds(0, chips)], 6)
+    drain(out.at[pl.ds(0, ncol - 1)], 4)
+    drain(out.at[pl.ds(0, chips - 1)], 2)
+    drain(out.at[pl.ds(0, ncol - 1)], 0)
+
+
+def merged(children, inverse, nrow, ncol):
+    rows_dev = children.shape[1]
     chunk = WIDE // nrow
     half = nrow // 2
+    piece = jax.ShapeDtypeStruct((2, rows_dev, WIDE), F32)
+    slices = pltpu.VMEM((ncol, 2, rows_dev // ncol, WIDE), F32)
     return pl.pallas_call(
-        functools.partial(reduce_kernel, nrow, ncol),
+        functools.partial(merge_kernel, nrow, ncol),
         out_shape=(
+            piece,
+            piece,
             jax.ShapeDtypeStruct((nrow, chunk, WIDE), F32),
             jax.ShapeDtypeStruct((WIDE, WIDE), F32),
         ),
-        in_specs=[VMEM, VMEM],
-        out_specs=(VMEM, VMEM),
+        in_specs=[SMEM, VMEM],
+        out_specs=(VMEM, VMEM, VMEM, VMEM),
         scratch_shapes=[
+            slices,
+            slices,
             pltpu.VMEM((WIDE, WIDE), F32),
             pltpu.VMEM((WIDE, WIDE), F32),
             pltpu.VMEM((nrow, 8, 128), F32),
@@ -335,14 +316,14 @@
             pltpu.VMEM((half, chunk, WIDE), F32),
             pltpu.VMEM((128, 128), F32),
             pltpu.VMEM((128, 128), F32),
-            pltpu.SemaphoreType.DMA((6,)),
+            pltpu.SemaphoreType.DMA((16,)),
             pltpu.SemaphoreType.DMA((2, 4 * half)),
         ],
         compiler_params=pltpu.CompilerParams(
-            collective_id=1, has_side_effects=True, vmem_limit_bytes=48 << 20
+            collective_id=0, has_side_effects=True, vmem_limit_bytes=48 << 20
         ),
-        name="reduce_and_factor",
-    )(front, panel)
+        name="merge",
+    )(inverse, children)
 
 
 def finish_kernel(front_ref, panel_ref, s_ref, linv_ref, rows_ref, trail_ref):
@@ -378,8 +359,7 @@
 def per_device(children, block_maps):
     ncol = lax.axis_size("col")
     nrow = lax.axis_size("row")
-    front, panel = exchange(children, inverted(block_maps), ncol)
-    s, linv = reduced(front, panel, nrow, ncol)
+    front, panel, s, linv = merged(children, inverted(block_maps), nrow, ncol)
     return finish(front, panel, s, linv)
 
 

time: 162 us -> 133 us (0.82)
  Pallas kernels: 159 us -> 129 us
    pallas_call x2 -> x1, Pallas kernels: 155 us -> 125 us  [merged(): pl.pallas_call(functools.partial(merge_kernel, nrow, ncol), out_shape=(pi...]
where the time goes in v2:
time: 133 us; the launch traced here: 131 us
  Pallas kernels  129 us (97%)
    pallas_call x1, Pallas kernels, merged(): pl.pallas_call(functools.partial(merge_kernel, nrow, ncol), out_shape=(pi...  125 us
    pallas_call x1, Pallas kernels, finish(): pl.pallas_call(finish_kernel, out_shape=(jax.ShapeDtypeStruct((WIDE, WIDE...  3.81 us

profile of v2, /device:TPU:24, one launch (start us, length us, event | category | flops | bytes accessed | tf_op | source)
XLA Modules:
  0.0 131.2 jit_solution(2562465613871413798)
XLA Ops:
  0.6 0.8 select_reduce_fusion.inv_ref
  1.4 0.0 copy-start
  1.4 1.2 copy-done
  2.6 124.7 %merge.1 = (f32[2,256,512]{2,1,0:T(8,128)S(1)}, f32[2,256,512]{2,1,0:T(8,128)S(1)}, f32[16,32,512]{2,1,0:T(8,128)S(1)}, f32[512,512]{1,0:T(8,128)S(1)}) custom-call(s32[2,64]{1,0:T(2,128)S(1)} %select_reduce_fusion.inv_ref, f32[2,256,512]{2,1,0:T(8,128)S(1)} %copy-done), custom_call_target="tpu_custom_call" | custom-call | tf_op jit(solution)/shard_map/merge/pallas_call | solution.py:298
  127.4 3.8 %finish.1 = (f32[512,512]{1,0:T(8,128)}, f32[2,256,512]{2,1,0:T(8,128)}) custom-call(f32[2,256,512]{2,1,0:T(8,128)S(1)} %get-tuple-element.6.front_ref, f32[2,256,512]{2,1,0:T(8,128)S(1)} %get-tuple-element.7.panel_ref, f32[16,32,512]{2,1,0:T(8,128)S(1)} %get-tuple-element.8.s_ref, f32[512,512]{1,0:T(8,128)S(1)} %get-tuple-element.9.linv_ref), custom_call_target="tpu_custom_call" | custom-call | tf_op jit(solution)/shard_map/finish/pallas_call | solution.py:339
Async XLA Ops:
  1.4 1.2 copy-start

commit v3 on v2

v3 whole, which is shorter than its diff:
```python
import functools
import math

import jax
import jax.numpy as jnp
from jax import lax
from jax.experimental import pallas as pl
from jax.experimental.pallas import tpu as pltpu
from jax.sharding import PartitionSpec as P

PANEL = 256
WIDE = 2 * PANEL
F32 = jnp.float32
BF16 = jnp.bfloat16
MESH = pl.DeviceIdType.MESH
VMEM = pl.BlockSpec(memory_space=pltpu.VMEM)
SMEM = pl.BlockSpec(memory_space=pltpu.SMEM)


def split(x):
    high = x.astype(BF16)
    low = (x - high.astype(F32)).astype(BF16)
    return high, low


def product(a, b, dims=((1,), (0,))):
    def one(x, y):
        return lax.dot_general(x, y, (dims, ((), ())), preferred_element_type=F32)

    return one(a[0], b[0]) + (one(a[0], b[1]) + one(a[1], b[0]))


DEEP = 16


def eliminate(gram, linv, k):
    groups = DEEP // 8
    top = pl.multiple_of(DEEP * k, DEEP)
    rows = [gram[pl.ds(top + 8 * g, 8), :] for g in range(groups)]
    invs = [linv[pl.ds(top + 8 * g, 8), :] for g in range(groups)]
    cols = []
    for g in range(groups):
        turned = pltpu.roll(rows[g], lax.rem(128 - DEEP * k, 128), axis=1)
        cols.append([jnp.broadcast_to(turned[:, j : j + 1], (8, 128)) for j in range(DEEP)])
    sub = lax.broadcasted_iota(jnp.int32, (8, 128), 0)

    def spread(value, i):
        return jnp.broadcast_to(value[i : i + 1, :], (8, 128))

    for p in range(DEEP):
        home, i = divmod(p, 8)
        pivot = spread(cols[home][p], i)
        recip = 1.0 / pivot
        mult = {}
        for g in range(home, groups):
            mult[g] = cols[g][p] * recip
        mult[home] = jnp.where(sub > i, mult[home], 0.0)
        for j in range(p + 1, DEEP):
            across = spread(cols[j // 8][p], j % 8)
            for g in range(j // 8, groups):
                cols[g][j] = cols[g][j] - mult[g] * across
        row, inv = spread(rows[home], i), spread(invs[home], i)
        for g in range(home, groups):
            rows[g] = rows[g] - mult[g] * row
            invs[g] = invs[g] - mult[g] * inv
        scale = jnp.where(sub == i, lax.rsqrt(pivot), 1.0)
        rows[home] = rows[home] * scale
        invs[home] = invs[home] * scale
    both = jnp.concatenate([jnp.concatenate(rows, axis=0), jnp.concatenate(invs, axis=0)], axis=1)
    gram[pl.ds(top, DEEP), :] = both[:, :128]
    linv[pl.ds(top, DEEP), :] = both[:, 128:]
    high, low = split(both)
    left = jnp.concatenate([high[:, :128], low[:, :128], high[:, :128]], axis=0)
    update = lax.dot_general(
        left,
        jnp.concatenate([high, high, low], axis=0),
        (((0,), (0,)), ((), ())),
        preferred_element_type=F32,
    )
    below = lax.broadcasted_iota(jnp.int32, (128, 128), 0) >= top + DEEP
    gram[...] = gram[...] - jnp.where(below, update[:, :128], 0.0)
    linv[...] = linv[...] - jnp.where(below, update[:, 128:], 0.0)


def orders(ncol):
    side = math.isqrt(ncol // 2)
    span = [(x, y, c) for x in range(side) for y in range(side) for c in range(2)]

    def far(o):
        return min(o[0], side - o[0]) + min(o[1], side - o[1])

    every = sorted(span[1:], key=lambda o: -far(o))
    return every, [o for o in every if o[2] == 0]


def merge_kernel(
    nrow, ncol, inv_ref, kids_ref, front_ref, panel_ref, s_ref, linv_ref,
    got, out, local, gram, tiles, part, pair_down, pair_up, sum_down, sum_up, diag, dinv, sems, ring
):
    me = lax.axis_index("col")
    mz = lax.axis_index("row")
    rows = kids_ref.shape[1] // ncol
    strip = WIDE // ncol
    chunk = WIDE // nrow
    ntile = strip // 8 * (WIDE // 128)
    core = lax.rem(me, 2)
    twin = me + 1 - 2 * core
    chips = ncol // 2
    side = math.isqrt(chips)
    mx, my = me // (2 * side), lax.rem(me // 2, side)
    every, same = orders(ncol)

    def peer(offset):
        x, y, c = offset
        x, y, c = lax.rem(mx + x, side), lax.rem(my + y, side), lax.rem(core + c, 2)
        return (x * side + y) * 2 + c

    barrier = pltpu.get_barrier_semaphore()

    @pl.loop(1, ncol)
    def _(d):
        pl.semaphore_signal(barrier, inc=1, device_id={"col": lax.rem(me + d, ncol)}, device_id_type=MESH)

    @pl.loop(1, nrow)
    def _(d):
        pl.semaphore_signal(barrier, inc=1, device_id={"row": lax.rem(mz + d, nrow)}, device_id_type=MESH)

    pl.semaphore_wait(barrier, ncol + nrow - 2)

    def send(src, dst, phase, to):
        pltpu.make_async_remote_copy(
            src_ref=src,
            dst_ref=dst,
            send_sem=sems.at[2 * phase],
            recv_sem=sems.at[2 * phase + 1],
            device_id=to,
            device_id_type=MESH,
        ).start()

    def drain(ref, which):
        pltpu.make_async_copy(ref, ref, sems.at[which]).wait()

    def slab(owner):
        return pl.ds(pl.multiple_of(owner * rows, rows), rows)

    def strip_of(owner):
        return pl.ds(pl.multiple_of(owner * strip, strip), strip)

    for offset in every:
        to = peer(offset)
        send(kids_ref.at[:, slab(to), :], got.at[me], 0, {"col": to})

    got[me] = kids_ref[:, slab(me), :]
    drain(got.at[pl.ds(0, ncol - 1)], 1)

    def place(to):
        for child in range(2):
            for half in range(2):
                block = inv_ref[child, 2 * to + half]
                pair = got[block // 2, child]
                low = jnp.broadcast_to(lax.rem(block, 2), (rows, PANEL)) == 0
                out[to, child, :, half * PANEL : (half + 1) * PANEL] = jnp.where(
                    low, pair[:, :PANEL], pair[:, PANEL:]
                )

    place(0)

    for offset in same:
        send(out.at[0], panel_ref.at[:, slab(me), :], 1, {"col": peer(offset)})

    panel_ref[:, slab(me), :] = out[0]

    @pl.loop(1, ncol)
    def _(to):
        place(to)

    for offset in every:
        to = peer(offset)
        send(out.at[to], front_ref.at[:, slab(me), :], 2, {"col": to})

    front_ref[:, slab(me), :] = out[me]
    drain(out.at[pl.ds(0, chips - 1)], 3)

    @pl.loop(0, chips)
    def _(i):
        here = panel_ref.at[:, slab(2 * i + core), :]
        send(here, here, 3, {"col": twin})

    drain(out.at[pl.ds(0, chips)], 7)

    pan = panel_ref[...].reshape(-1, WIDE)
    pan_t = split(pan.T)
    local[...] = product(pan_t, split(pan))

    def tile_at(z):
        t = lax.rem(z, ntile)
        top = me * strip + (t // 4) * 8
        return pl.ds(pl.multiple_of(top, 8), 8), pl.ds(pl.multiple_of(lax.rem(t, 4) * 128, 128), 128)

    @pl.loop(1, nrow)
    def _(d):
        to = lax.rem(mz + d, nrow)
        r, c = tile_at(to)
        send(local.at[r, c], tiles.at[mz], 4, {"row": to})

    r, c = tile_at(mz)
    tiles[mz] = local[r, c]
    drain(tiles.at[pl.ds(0, nrow - 1)], 9)
    total = tiles[0]
    for z in range(1, nrow):
        total = total + tiles[z]
    gram[r, c] = total
    for d in range(-(ntile // 2), ntile // 2):
        if d:
            send(gram.at[r, c], gram.at[r, c], 5, {"row": lax.rem(mz + d + nrow, nrow)})

    half = nrow // 2
    last = half // 2 - 1

    def at(offset):
        return lax.rem(mz + offset + 2 * nrow, nrow)

    def copy(src, dst, index, u, hops):
        return pltpu.make_async_remote_copy(
            src_ref=src, dst_ref=dst, send_sem=ring.at[0, index, u], recv_sem=ring.at[1, index, u],
            device_id={"row": at(hops)}, device_id_type=MESH,
        )

    def pairs_down(k, u):
        return copy(part.at[at(2 * k - half), u], pair_down.at[k, u], k, u, -1)

    def pairs_up(k, u):
        return copy(part.at[at(half - 2 - 2 * k), u], pair_up.at[k, u], 4 + k, u, 1)

    def chain_down(k, u):
        return copy(pair_down.at[k, u], sum_down.at[k, u], 8 + k, u, -2 if k < last else -1)

    def chain_up(k, u):
        src = pair_up.at[k - 1, u] if k else part.at[at(half - 1), u]
        return copy(src, sum_up.at[k, u], 12 + k, u, 2 if k < last else 1)

    def share_up(k, u):
        here = s_ref.at[at(1 - 2 * k if k else 0), u]
        return copy(here, here, 16 + k, u, 2 if k else 1)

    def aside_up(k, u):
        here = s_ref.at[at(-2 * k - 1), u]
        return copy(here, here, 20 + k, u, 1)

    def share_down(k, u):
        here = s_ref.at[at(2 * k - 1 if k else 0), u]
        return copy(here, here, 24 + k, u, -2 if k else -1)

    def aside_down(k, u):
        here = s_ref.at[at(2 * k + 1), u]
        return copy(here, here, 28 + k, u, -1)

    def ring_start(u):
        for k in range(last + 1):
            pairs_down(k, u).start()
            if k == 0:
                chain_up(0, u).start()
            if k < last:
                pairs_up(k, u).start()

    def ring_sum(k, u):
        pairs_down(k, u).wait_recv()
        value = pair_down[k, u] + part[at(2 * k + 1 - half), u]
        if k:
            chain_down(k - 1, u).wait_recv()
            value = value + sum_down[k - 1, u]
        pair_down[k, u] = value
        chain_down(k, u).start()
        if k:
            pairs_up(k - 1, u).wait_recv()
            chain_up(k - 1, u).wait_recv()
            pair_up[k - 1, u] = pair_up[k - 1, u] + part[at(half - 1 - 2 * k), u] + sum_up[k - 1, u]
            chain_up(k, u).start()

    def ring_turn(u):
        chain_down(last, u).wait_recv()
        chain_up(last, u).wait_recv()
        s_ref[mz, u] = part[mz, u] + sum_down[last, u] + sum_up[last, u]
        share_up(0, u).start()
        share_down(0, u).start()

    def ring_share(k, u):
        share_up(k, u).wait_recv()
        if k < last:
            share_up(k + 1, u).start()
        aside_up(k, u).start()
        share_down(k, u).wait_recv()
        if k < last:
            share_down(k + 1, u).start()
            aside_down(k, u).start()

    def ring_end(u):
        for k in range(last + 1):
            aside_up(k, u).wait_recv()
            if k < last:
                aside_down(k, u).wait_recv()

    both = range(2)
    points = [functools.partial(ring_sum, k, u) for k in range(last + 1) for u in both]
    points += [functools.partial(ring_turn, u) for u in both]
    points += [functools.partial(ring_share, k, u) for k in range(last + 1) for u in both]

    drain(out.at[pl.ds(0, ncol - 1)], 5)
    fr = split(front_ref[...].reshape(-1, WIDE))
    for u in both:
        columns = slice(u * PANEL, (u + 1) * PANEL)
        part[:, u] = product(pan_t, (fr[0][:, columns], fr[1][:, columns])).reshape(nrow, chunk, PANEL)
        ring_start(u)

    drain(tiles.at[pl.ds(0, ntile - 1)], 11)
    for offset in same:
        here = gram.at[strip_of(me), :]
        send(here, here, 6, {"col": peer(offset)})
    for _ in range(4):
        points.pop(0)()
    drain(out.at[pl.ds(0, chips - 1)], 13)

    @pl.loop(0, chips)
    def _(i):
        here = gram.at[strip_of(2 * i + core), :]
        send(here, here, 7, {"col": twin})

    drain(out.at[pl.ds(0, chips)], 15)
    drain(out.at[pl.ds(0, chips)], 14)
    drain(out.at[pl.ds(0, chips - 1)], 12)
    drain(tiles.at[pl.ds(0, ntile - 1)], 10)
    linv_ref[...] = jnp.zeros((WIDE, WIDE), F32)
    row_id = lax.broadcasted_iota(jnp.int32, (128, 128), 0)
    col_id = lax.broadcasted_iota(jnp.int32, (128, 128), 1)
    eye = jnp.where(row_id == col_id, 1.0, 0.0)
    for ob in range(WIDE // 128):
        lo, hi = 128 * ob, 128 * (ob + 1)
        diag[...] = gram[lo:hi, lo:hi]
        dinv[...] = eye
        for quarter in range(4):
            count = 32 // DEEP

            @pl.loop(0, count)
            def _(i):
                eliminate(diag, dinv, count * quarter + i)

            if points:
                points.pop(0)()
        lower = jnp.where(row_id >= col_id, dinv[...], 0.0)
        inv = split(lower)
        linv_ref[lo:hi, lo:hi] = lower
        if ob:
            linv_ref[lo:hi, :lo] = product(inv, split(linv_ref[lo:hi, :lo]))
        if hi < WIDE:
            right = product(inv, split(gram[lo:hi, hi:]))
            right_t = split(right.T)
            gram[hi:, hi:] = gram[hi:, hi:] - product(right_t, split(right))
            linv_ref[hi:, :hi] = linv_ref[hi:, :hi] - product(right_t, split(linv_ref[lo:hi, :hi]))
    while points:
        points.pop(0)()
    for u in both:
        ring_end(u)
    for u in both:
        for k in range(last + 1):
            for move in (pairs_down, chain_down, chain_up, share_up, aside_up, share_down):
                move(k, u).wait_send()
            if k < last:
                pairs_up(k, u).wait_send()
                aside_down(k, u).wait_send()
    drain(tiles.at[pl.ds(0, nrow - 1)], 8)
    drain(out.at[pl.ds(0, chips)], 6)
    drain(out.at[pl.ds(0, ncol - 1)], 4)
    drain(out.at[pl.ds(0, chips - 1)], 2)
    drain(out.at[pl.ds(0, ncol - 1)], 0)


def merged(children, inverse, nrow, ncol):
    rows_dev = children.shape[1]
    chunk = WIDE // nrow
    quarter = nrow // 4
    piece = jax.ShapeDtypeStruct((2, rows_dev, WIDE), F32)
    slices = pltpu.VMEM((ncol, 2, rows_dev // ncol, WIDE), F32)
    return pl.pallas_call(
        functools.partial(merge_kernel, nrow, ncol),
        out_shape=(
            piece,
            piece,
            jax.ShapeDtypeStruct((nrow, 2, chunk, PANEL), F32),
            jax.ShapeDtypeStruct((WIDE, WIDE), F32),
        ),
        in_specs=[SMEM, VMEM],
        out_specs=(VMEM, VMEM, VMEM, VMEM),
        scratch_shapes=[
            slices,
            slices,
            pltpu.VMEM((WIDE, WIDE), F32),
            pltpu.VMEM((WIDE, WIDE), F32),
            pltpu.VMEM((nrow, 8, 128), F32),
            pltpu.VMEM((nrow, 2, chunk, PANEL), F32),
            pltpu.VMEM((quarter, 2, chunk, PANEL), F32),
            pltpu.VMEM((quarter - 1, 2, chunk, PANEL), F32),
            pltpu.VMEM((quarter, 2, chunk, PANEL), F32),
            pltpu.VMEM((quarter, 2, chunk, PANEL), F32),
            pltpu.VMEM((128, 128), F32),
            pltpu.VMEM((128, 128), F32),
            pltpu.SemaphoreType.DMA((16,)),
            pltpu.SemaphoreType.DMA((2, 32, 2)),
        ],
        compiler_params=pltpu.CompilerParams(
            collective_id=0, has_side_effects=True, vmem_limit_bytes=48 << 20
        ),
        name="merge",
    )(inverse, children)


def finish_kernel(front_ref, panel_ref, s_ref, linv_ref, rows_ref, trail_ref):
    inv = split(linv_ref[...])
    summed = jnp.concatenate([s_ref[:, u].reshape(WIDE, PANEL) for u in range(2)], axis=1)
    upper = product(inv, split(summed))
    rows_ref[...] = upper
    back = product(split(linv_ref[...].T), split(upper))
    pan = panel_ref[...].reshape(-1, WIDE)
    trail_ref[...] = front_ref[...] - product(split(pan), split(back)).reshape(front_ref.shape)


def finish(front, panel, s, linv):
    return pl.pallas_call(
        finish_kernel,
        out_shape=(
            jax.ShapeDtypeStruct((WIDE, WIDE), F32),
            jax.ShapeDtypeStruct(front.shape, F32),
        ),
        in_specs=[VMEM] * 4,
        out_specs=(VMEM, VMEM),
        compiler_params=pltpu.CompilerParams(vmem_limit_bytes=48 << 20),
        name="finish",
    )(front, panel, s, linv)


def inverted(maps):
    count = maps.shape[1]
    ids = lax.broadcasted_iota(jnp.int32, (2, count, count), 1)
    hit = maps[:, :, None] == lax.broadcasted_iota(jnp.int32, (2, count, count), 2)
    return jnp.sum(jnp.where(hit, ids, 0), axis=1)


def per_device(children, block_maps):
    ncol = lax.axis_size("col")
    nrow = lax.axis_size("row")
    front, panel, s, linv = merged(children, inverted(block_maps), nrow, ncol)
    return finish(front, panel, s, linv)


def solution(mesh):
    placed = (P(None, "row", "col"), P())
    return jax.shard_map(
        per_device,
        mesh=mesh,
        in_specs=placed,
        out_specs=(P(None, "col"), P(None, "row", "col")),
        check_vma=False,
    )
```

time: 133 us -> 111 us (0.83)
  the two profiles are of different devices: /device:TPU:24 before, /device:TPU:2 now
where the time goes in v3:
time: 111 us; the launch traced here: 110 us
  Pallas kernels  108 us (97%)
  local copies, waits for them, and re-layouts  1.22 us (1%)
    pallas_call x1, Pallas kernels, merged(): pl.pallas_call(functools.partial(merge_kernel, nrow, ncol), out_shape=(pi...  104 us
    pallas_call x1, Pallas kernels, finish(): pl.pallas_call(finish_kernel, out_shape=(jax.ShapeDtypeStruct((WIDE, WIDE...  3.81 us

profile of v3, /device:TPU:2, one launch (start us, length us, event | category | flops | bytes accessed | tf_op | source)
XLA Modules:
  0.0 110.5 jit_solution(12633650650906876859)
XLA Ops:
  0.6 0.8 select_reduce_fusion.inv_ref
  1.4 0.0 copy-start
  1.4 1.2 %copy-done = f32[2,256,512]{2,1,0:T(8,128)S(1)} copy-done((f32[2,256,512]{2,1,0:T(8,128)S(1)}, f32[2,256,512]{2,1,0:T(8,128)}, u32[]{:S(2)}) %copy-start) | copy-done | bytes 1048600
  2.6 104.0 %merge.1 = (f32[2,256,512]{2,1,0:T(8,128)S(1)}, f32[2,256,512]{2,1,0:T(8,128)S(1)}, f32[16,2,32,256]{3,2,1,0:T(8,128)S(1)}, f32[512,512]{1,0:T(8,128)S(1)}) custom-call(s32[2,64]{1,0:T(2,128)S(1)} %select_reduce_fusion.inv_ref, f32[2,256,512]{2,1,0:T(8,128)S(1)} %copy-done), custom_call_target="tpu_custom_call" | custom-call | tf_op jit(solution)/shard_map/merge/pallas_call | solution.py:383
  106.7 3.8 %finish.1 = (f32[512,512]{1,0:T(8,128)}, f32[2,256,512]{2,1,0:T(8,128)}) custom-call(f32[2,256,512]{2,1,0:T(8,128)S(1)} %get-tuple-element.6.front_ref, f32[2,256,512]{2,1,0:T(8,128)S(1)} %get-tuple-element.7.panel_ref, f32[16,2,32,256]{3,2,1,0:T(8,128)S(1)} %get-tuple-element.8.s_ref, f32[512,512]{1,0:T(8,128)S(1)} %get-tuple-element.9.linv_ref), custom_call_target="tpu_custom_call" | custom-call | tf_op jit(solution)/shard_map/finish/pallas_call | solution.py:427
Async XLA Ops:
  1.4 1.2 %copy-start = (f32[2,256,512]{2,1,0:T(8,128)S(1)}, f32[2,256,512]{2,1,0:T(8,128)}, u32[]{:S(2)}) copy-start(f32[2,256,512]{2,1,0:T(8,128)} %kids_ref.1) | copy-start | bytes 3145732

commit v4 on v3

--- a/solution.py
+++ b/solution.py
@@ -94,8 +94,8 @@
 
 
 def merge_kernel(
-    nrow, ncol, inv_ref, kids_ref, front_ref, panel_ref, s_ref, linv_ref,
-    got, out, local, gram, tiles, part, pair_down, pair_up, sum_down, sum_up, diag, dinv, sems, ring
+    nrow, ncol, inv_ref, kids_ref, front_ref, basis_ref, s_ref, linv_ref,
+    panel_ref, got, out, local, gram, tiles, part, pair_down, pair_up, sum_down, sum_up, diag, dinv, sems, ring, known
 ):
     me = lax.axis_index("col")
     mz = lax.axis_index("row")
@@ -121,11 +121,14 @@
     def _(d):
         pl.semaphore_signal(barrier, inc=1, device_id={"col": lax.rem(me + d, ncol)}, device_id_type=MESH)
 
-    @pl.loop(1, nrow)
-    def _(d):
-        pl.semaphore_signal(barrier, inc=1, device_id={"row": lax.rem(mz + d, nrow)}, device_id_type=MESH)
-
-    pl.semaphore_wait(barrier, ncol + nrow - 2)
+    def greet(semaphore, hops):
+        for d in (hops, nrow - hops):
+            pl.semaphore_signal(
+                semaphore, inc=1, device_id={"row": lax.rem(mz + d, nrow)}, device_id_type=MESH
+            )
+
+    greet(barrier, 1)
+    pl.semaphore_wait(barrier, ncol + 1)
 
     def send(src, dst, phase, to):
         pltpu.make_async_remote_copy(
@@ -151,6 +154,11 @@
         send(kids_ref.at[:, slab(to), :], got.at[me], 0, {"col": to})
 
     got[me] = kids_ref[:, slab(me), :]
+    hops = 1
+    for level in range(3):
+        greet(known.at[level], hops)
+        pl.semaphore_wait(known.at[level], 2)
+        hops *= 2
     drain(got.at[pl.ds(0, ncol - 1)], 1)
 
     def place(to):
@@ -159,36 +167,36 @@
                 block = inv_ref[child, 2 * to + half]
                 pair = got[block // 2, child]
                 low = jnp.broadcast_to(lax.rem(block, 2), (rows, PANEL)) == 0
-                out[to, child, :, half * PANEL : (half + 1) * PANEL] = jnp.where(
-                    low, pair[:, :PANEL], pair[:, PANEL:]
-                )
+                out[to, half, child] = jnp.where(low, pair[:, :PANEL], pair[:, PANEL:])
 
     place(0)
 
     for offset in same:
-        send(out.at[0], panel_ref.at[:, slab(me), :], 1, {"col": peer(offset)})
-
-    panel_ref[:, slab(me), :] = out[0]
+        send(out.at[0], panel_ref.at[:, :, slab(me), :], 1, {"col": peer(offset)})
+
+    panel_ref[:, :, slab(me), :] = out[0]
 
     @pl.loop(1, ncol)
     def _(to):
         place(to)
 
-    for offset in every:
-        to = peer(offset)
-        send(out.at[to], front_ref.at[:, slab(me), :], 2, {"col": to})
-
-    front_ref[:, slab(me), :] = out[me]
+    for half in range(2):
+        columns = slice(half * PANEL, (half + 1) * PANEL)
+        for offset in every:
+            to = peer(offset)
+            send(out.at[to, half], front_ref.at[:, slab(me), columns], (2, 8)[half], {"col": to})
+        front_ref[:, slab(me), columns] = out[me, half]
+
     drain(out.at[pl.ds(0, chips - 1)], 3)
 
     @pl.loop(0, chips)
     def _(i):
-        here = panel_ref.at[:, slab(2 * i + core), :]
+        here = panel_ref.at[:, :, slab(2 * i + core), :]
         send(here, here, 3, {"col": twin})
 
     drain(out.at[pl.ds(0, chips)], 7)
 
-    pan = panel_ref[...].reshape(-1, WIDE)
+    pan = jnp.concatenate([panel_ref[u].reshape(-1, PANEL) for u in range(2)], axis=1)
     pan_t = split(pan.T)
     local[...] = product(pan_t, split(pan))
 
@@ -205,15 +213,6 @@
 
     r, c = tile_at(mz)
     tiles[mz] = local[r, c]
-    drain(tiles.at[pl.ds(0, nrow - 1)], 9)
-    total = tiles[0]
-    for z in range(1, nrow):
-        total = total + tiles[z]
-    gram[r, c] = total
-    for d in range(-(ntile // 2), ntile // 2):
-        if d:
-            send(gram.at[r, c], gram.at[r, c], 5, {"row": lax.rem(mz + d + nrow, nrow)})
-
     half = nrow // 2
     last = half // 2 - 1
 
@@ -255,13 +254,12 @@
         here = s_ref.at[at(2 * k + 1), u]
         return copy(here, here, 28 + k, u, -1)
 
-    def ring_start(u):
-        for k in range(last + 1):
-            pairs_down(k, u).start()
-            if k == 0:
-                chain_up(0, u).start()
-            if k < last:
-                pairs_up(k, u).start()
+    def ring_start(k, u):
+        pairs_down(k, u).start()
+        if k == 0:
+            chain_up(0, u).start()
+        if k < last:
+            pairs_up(k, u).start()
 
     def ring_sum(k, u):
         pairs_down(k, u).wait_recv()
@@ -305,18 +303,29 @@
     points += [functools.partial(ring_turn, u) for u in both]
     points += [functools.partial(ring_share, k, u) for k in range(last + 1) for u in both]
 
-    drain(out.at[pl.ds(0, ncol - 1)], 5)
-    fr = split(front_ref[...].reshape(-1, WIDE))
     for u in both:
         columns = slice(u * PANEL, (u + 1) * PANEL)
-        part[:, u] = product(pan_t, (fr[0][:, columns], fr[1][:, columns])).reshape(nrow, chunk, PANEL)
-        ring_start(u)
-
+        drain(out.at[pl.ds(0, ncol - 1), 0], (5, 17)[u])
+        fr = split(front_ref[:, :, columns].reshape(-1, PANEL))
+        part[:, u] = product(pan_t, fr).reshape(nrow, chunk, PANEL)
+        ring_start(0, u)
+
+    drain(tiles.at[pl.ds(0, nrow - 1)], 9)
+    total = tiles[0]
+    for z in range(1, nrow):
+        total = total + tiles[z]
+    gram[r, c] = total
+    for d in range(-(ntile // 2), ntile // 2):
+        if d:
+            send(gram.at[r, c], gram.at[r, c], 5, {"row": lax.rem(mz + d + nrow, nrow)})
+    for k in range(1, last + 1):
+        for u in both:
+            ring_start(k, u)
     drain(tiles.at[pl.ds(0, ntile - 1)], 11)
     for offset in same:
         here = gram.at[strip_of(me), :]
         send(here, here, 6, {"col": peer(offset)})
-    for _ in range(4):
+    for _ in range(6):
         points.pop(0)()
     drain(out.at[pl.ds(0, chips - 1)], 13)
 
@@ -356,6 +365,11 @@
             right_t = split(right.T)
             gram[hi:, hi:] = gram[hi:, hi:] - product(right_t, split(right))
             linv_ref[hi:, :hi] = linv_ref[hi:, :hi] - product(right_t, split(linv_ref[lo:hi, :hi]))
+    if points:
+        points.pop(0)()
+    factor_t = split(linv_ref[...].T)
+    pan = jnp.concatenate([panel_ref[u].reshape(-1, PANEL) for u in range(2)], axis=1)
+    basis_ref[...] = product(split(pan), factor_t).reshape(basis_ref.shape)
     while points:
         points.pop(0)()
     for u in both:
@@ -369,7 +383,8 @@
                 aside_down(k, u).wait_send()
     drain(tiles.at[pl.ds(0, nrow - 1)], 8)
     drain(out.at[pl.ds(0, chips)], 6)
-    drain(out.at[pl.ds(0, ncol - 1)], 4)
+    drain(out.at[pl.ds(0, ncol - 1), 0], 4)
+    drain(out.at[pl.ds(0, ncol - 1), 1], 16)
     drain(out.at[pl.ds(0, chips - 1)], 2)
     drain(out.at[pl.ds(0, ncol - 1)], 0)
 
@@ -379,7 +394,6 @@
     chunk = WIDE // nrow
     quarter = nrow // 4
     piece = jax.ShapeDtypeStruct((2, rows_dev, WIDE), F32)
-    slices = pltpu.VMEM((ncol, 2, rows_dev // ncol, WIDE), F32)
     return pl.pallas_call(
         functools.partial(merge_kernel, nrow, ncol),
         out_shape=(
@@ -391,8 +405,9 @@
         in_specs=[SMEM, VMEM],
         out_specs=(VMEM, VMEM, VMEM, VMEM),
         scratch_shapes=[
-            slices,
-            slices,
+            pltpu.VMEM((2, 2, rows_dev, PANEL), F32),
+            pltpu.VMEM((ncol, 2, rows_dev // ncol, WIDE), F32),
+            pltpu.VMEM((ncol, 2, 2, rows_dev // ncol, PANEL), F32),
             pltpu.VMEM((WIDE, WIDE), F32),
             pltpu.VMEM((WIDE, WIDE), F32),
             pltpu.VMEM((nrow, 8, 128), F32),
@@ -403,8 +418,9 @@
             pltpu.VMEM((quarter, 2, chunk, PANEL), F32),
             pltpu.VMEM((128, 128), F32),
             pltpu.VMEM((128, 128), F32),
-            pltpu.SemaphoreType.DMA((16,)),
+            pltpu.SemaphoreType.DMA((18,)),
             pltpu.SemaphoreType.DMA((2, 32, 2)),
+            pltpu.SemaphoreType.REGULAR((3,)),
         ],
         compiler_params=pltpu.CompilerParams(
             collective_id=0, has_side_effects=True, vmem_limit_bytes=48 << 20
@@ -413,17 +429,15 @@
     )(inverse, children)
 
 
-def finish_kernel(front_ref, panel_ref, s_ref, linv_ref, rows_ref, trail_ref):
-    inv = split(linv_ref[...])
+def finish_kernel(front_ref, basis_ref, s_ref, linv_ref, rows_ref, trail_ref):
     summed = jnp.concatenate([s_ref[:, u].reshape(WIDE, PANEL) for u in range(2)], axis=1)
-    upper = product(inv, split(summed))
+    upper = product(split(linv_ref[...]), split(summed))
     rows_ref[...] = upper
-    back = product(split(linv_ref[...].T), split(upper))
-    pan = panel_ref[...].reshape(-1, WIDE)
-    trail_ref[...] = front_ref[...] - product(split(pan), split(back)).reshape(front_ref.shape)
-
-
-def finish(front, panel, s, linv):
+    basis = split(basis_ref[...].reshape(-1, WIDE))
+    trail_ref[...] = front_ref[...] - product(basis, split(upper)).reshape(front_ref.shape)
+
+
+def finish(front, basis, s, linv):
     return pl.pallas_call(
         finish_kernel,
         out_shape=(
@@ -434,7 +448,7 @@
         out_specs=(VMEM, VMEM),
         compiler_params=pltpu.CompilerParams(vmem_limit_bytes=48 << 20),
         name="finish",
-    )(front, panel, s, linv)
+    )(front, basis, s, linv)
 
 
 def inverted(maps):
@@ -447,8 +461,8 @@
 def per_device(children, block_maps):
     ncol = lax.axis_size("col")
     nrow = lax.axis_size("row")
-    front, panel, s, linv = merged(children, inverted(block_maps), nrow, ncol)
-    return finish(front, panel, s, linv)
+    front, basis, s, linv = merged(children, inverted(block_maps), nrow, ncol)
+    return finish(front, basis, s, linv)
 
 
 def solution(mesh):

time: 111 us -> 104 us (0.937)
  the two profiles are of different devices: /device:TPU:2 before, /device:TPU:24 now
where the time goes in v4:
time: 104 us; the launch traced here: 102 us
  Pallas kernels  99.3 us (95%)
  local copies, waits for them, and re-layouts  1.22 us (1%)
    pallas_call x1, Pallas kernels, merged(): pl.pallas_call(functools.partial(merge_kernel, nrow, ncol), out_shape=(pi...  96.4 us
    pallas_call x1, Pallas kernels, finish(): pl.pallas_call(finish_kernel, out_shape=(jax.ShapeDtypeStruct((WIDE, WIDE...  2.92 us

profile of v4, /device:TPU:24, one launch (start us, length us, event | category | flops | bytes accessed | tf_op | source)
XLA Modules:
  0.0 101.9 jit_solution(13313849105360070235)
XLA Ops:
  0.6 0.8 select_reduce_fusion.inv_ref
  1.4 0.0 copy-start
  1.4 1.2 %copy-done = f32[2,256,512]{2,1,0:T(8,128)S(1)} copy-done((f32[2,256,512]{2,1,0:T(8,128)S(1)}, f32[2,256,512]{2,1,0:T(8,128)}, u32[]{:S(2)}) %copy-start) | copy-done | bytes 1048600
  2.6 96.4 %merge.1 = (f32[2,256,512]{2,1,0:T(8,128)S(1)}, f32[2,256,512]{2,1,0:T(8,128)S(1)}, f32[16,2,32,256]{3,2,1,0:T(8,128)S(1)}, f32[512,512]{1,0:T(8,128)S(1)}) custom-call(s32[2,64]{1,0:T(2,128)S(1)} %select_reduce_fusion.inv_ref, f32[2,256,512]{2,1,0:T(8,128)S(1)} %copy-done), custom_call_target="tpu_custom_call" | custom-call | tf_op jit(solution)/shard_map/merge/pallas_call | solution.py:397
  99.0 2.9 %finish.1 = (f32[512,512]{1,0:T(8,128)}, f32[2,256,512]{2,1,0:T(8,128)}) custom-call(f32[2,256,512]{2,1,0:T(8,128)S(1)} %get-tuple-element.6.front_ref, f32[2,256,512]{2,1,0:T(8,128)S(1)} %get-tuple-element.7.basis_ref, f32[16,2,32,256]{3,2,1,0:T(8,128)S(1)} %get-tuple-element.8.s_ref, f32[512,512]{1,0:T(8,128)S(1)} %get-tuple-element.9.linv_ref), custom_call_target="tpu_custom_call" | custom-call | tf_op jit(solution)/shard_map/finish/pallas_call | solution.py:441
Async XLA Ops:
  1.4 1.2 %copy-start = (f32[2,256,512]{2,1,0:T(8,128)S(1)}, f32[2,256,512]{2,1,0:T(8,128)}, u32[]{:S(2)}) copy-start(f32[2,256,512]{2,1,0:T(8,128)} %kids_ref.1) | copy-start | bytes 3145732
